TPU v7x, 32 devices: a whole 2x2x4 slice. The times are simulated.
32 devices in a mesh: head: 2 (over y), ctx: 16 (over z, x, core).
Axes of the slice: x: 2, y: 2, z: 4, core: 2. Of those that a mesh axis runs over, the one named last changes fastest.
Arguments:
- queries: bfloat16 [512, 24576], P(None, 'head'), may hold values from -100 to 100
- attn_keys: bfloat16 [4096, 24576], P('ctx', 'head'), may hold values from -6 to 6
- index_queries: bfloat16 [512, 8192], P(None, 'head'), may hold values from -16 to 16
- index_keys: bfloat16 [4096, 128], P('ctx'), may hold values from -6 to 6
- head_weights: float32 [512, 64], P(None, 'head'), may hold values from 0.1 to 1
- query_pos: int32 [512], replicated, may hold values from 16 to 32767
- key_offset: int32 [4096], P('ctx'), may hold values from 0 to 7
Outputs:
- index_query_grad: float32 [512, 8192], P('ctx', 'head')
- index_key_grad: float32 [4096, 128], P('ctx')
All inputs are finite; a program needn't handle non-finite values.
Results may differ from a plain program's by a relative error of at most 0.0027.
Values sent between devices are 32-bit elements; how exact they have to be, the bound alone decides.
A program may use at most 128 MiB of HBM per device.

v0:
```python
import math
import jax
import jax.numpy as jnp
from jax import lax
from jax.sharding import PartitionSpec as P

HEADS = 128
HEAD_DIM = 192
IDIM = 128
STRIDE = 8
NEG_FILL = -1e30


def combined_all(part, axis, combine):
    gathered = jax.tree.map(lambda a: lax.all_gather(a, axis), part)

    def take(source):
        return jax.tree.map(lambda a: lax.dynamic_index_in_dim(a, source, 0, False), gathered)

    return lax.fori_loop(
        1, lax.axis_size(axis), lambda source, state: combine(state, take(source)), take(0)
    )


def combine_stats(earlier, later):
    top_value = jnp.maximum(earlier[0], later[0])
    total_mass = earlier[1] * jnp.exp(earlier[0] - top_value) + later[1] * jnp.exp(
        later[0] - top_value
    )
    return (top_value, total_mass)


def row_stats(values, visible):
    masked = jnp.where(visible, values, NEG_FILL)
    local_top = jnp.max(masked, axis=-1)
    local_mass = jnp.sum(jnp.where(visible, jnp.exp(masked - local_top[..., None]), 0.0), axis=-1)
    top_value, total_mass = combined_all((local_top, local_mass), "ctx", combine_stats)
    return jnp.where(visible, jnp.exp(masked - top_value[..., None]), 0.0) / total_mass[..., None]


def shards(queries, attn_keys, index_queries, index_keys, head_weights, query_pos, key_offset):
    query_rows = queries.shape[0]
    key_rows = attn_keys.shape[0]
    local_heads = attn_keys.shape[1] // HEAD_DIM
    index_heads = index_queries.shape[1] // IDIM
    key_start = lax.axis_index("ctx") * key_rows
    key_pos = STRIDE * (key_start + jnp.arange(key_rows, dtype=jnp.int32)) + key_offset
    visible = key_pos[None, :] <= query_pos[:, None]
    attn_scale = 1.0 / math.sqrt(HEAD_DIM)
    inv_scale = 1.0 / math.sqrt(IDIM)
    query_heads = queries.reshape(query_rows, local_heads, HEAD_DIM)
    key_heads = attn_keys.reshape(key_rows, local_heads, HEAD_DIM)
    scores = (
        jnp.einsum("thd,shd->hts", query_heads, key_heads, preferred_element_type=jnp.float32)
        * attn_scale
    )
    head_probs = row_stats(scores, visible[None])
    target_part = jnp.sum(head_probs, axis=0)
    index_heads_q = index_queries.reshape(query_rows, index_heads, IDIM)
    activation = (
        jnp.einsum("tjd,sd->tjs", index_heads_q, index_keys, preferred_element_type=jnp.float32)
        * inv_scale
    )
    logit_part = jnp.sum(head_weights[:, :, None] * jnp.maximum(activation, 0.0), axis=1)
    target = lax.psum(target_part, "head") / HEADS
    logits = lax.psum(logit_part, "head")
    prob_step = row_stats(logits, visible) - target
    grad_terms = jnp.where(
        activation > 0.0, prob_step[:, None, :] * head_weights[:, :, None] * inv_scale, 0.0
    ).astype(jnp.bfloat16)
    key_part = jnp.einsum(
        "tjs,tjd->sd", grad_terms, index_heads_q, preferred_element_type=jnp.float32
    )
    key_grad = lax.psum(key_part, "head")
    result = jnp.einsum("tjs,sd->tjd", grad_terms, index_keys, preferred_element_type=jnp.float32)
    query_grad = lax.psum_scatter(
        result.reshape(
            query_rows // lax.axis_size("ctx") * lax.axis_size("ctx"), index_heads * IDIM
        ),
        "ctx",
        scatter_dimension=0,
        tiled=True,
    )
    return (query_grad, key_grad)


def solution(mesh):
    in_specs = (
        P(None, "head"),
        P("ctx", "head"),
        P(None, "head"),
        P("ctx", None),
        P(None, "head"),
        P(),
        P("ctx"),
    )
    out_specs = (P("ctx", "head"), P("ctx", None))
    return jax.shard_map(shards, mesh=mesh, in_specs=in_specs, out_specs=out_specs, check_vma=False)
```

profile of v0, /device:TPU:0, one launch (start us, length us, event | category | flops | bytes accessed | tf_op | source)
XLA Modules:
  0.0 419.4 jit_solution(3195242327979125005)
XLA Ops:
  9.0 16.7 %copy.35 = bf16[512,12288]{0,1:T(8,128)(2,1)} copy(bf16[512,12288]{1,0:T(8,128)(2,1)} %param.11) | data formatting | bytes 25165824 | tf_op args[0]
  25.7 8.7 %copy.36 = bf16[256,12288]{0,1:T(8,128)(2,1)} copy(bf16[256,12288]{1,0:T(8,128)(2,1)} %param.12) | data formatting | bytes 12582912 | tf_op args[1]
  34.3 20.6 %fusion.3 = (f32[64,512]{1,0:T(8,128)S(1)}, f32[64,512,256]{1,2,0:T(8,128)}) fusion(pred[512,256]{0,1:T(8,128)(4,1)S(1)} %copy.34, bf16[512,64,192]{0,2,1:T(8,128)(2,1)} %bitcast.63, bf16[256,64,192]{0,2,1:T(8,128)(2,1)} %bitcast.65), kind=kOutput, calls=%fused_computation.12 | convolution fusion | flops 3246358528 | bytes 52690944 | tf_op jit(solution)/shard_map/thd,shd->hts/dot_general | solution.py:54
  55.0 15.6 %select_reduce_fusion = f32[64,512]{1,0:T(8,128)} fusion(f32[64,512,256]{1,2,0:T(8,128)} %get-tuple-element.303, f32[64,512]{1,0:T(8,128)S(1)} %get-tuple-element.302, pred[512,256]{0,1:T(8,128)(4,1)S(1)} %copy.34), kind=kLoop, calls=%fused_computation.9 | loop fusion | flops 41910272 | bytes 33947648 | tf_op jit(solution)/shard_map/reduce_sum | solution.py:36
  71.4 5.4 %convert_reduce_fusion = (u32[512,256]{1,0:T(8,128)S(1)}, f32[512,32,256]{2,0,1:T(8,128)S(1)}) fusion(bf16[256,128]{1,0:T(8,128)(2,1)S(1)} %copy-done, bf16[512,4096]{1,0:T(8,128)(2,1)} %param.13), kind=kOutput, calls=%fused_computation.14 | convolution fusion | flops 1094582272 | bytes 21561344 | tf_op jit(solution)/shard_map/tjd,sd->tjs/dot_general | solution.py:61
  76.8 3.7 multiply_reduce_fusion
  80.4 34.5 %all-gather.11.cloned.1.call-done = f32[1024,512]{1,0:T(8,128)} async-done(((f32[64,512]{1,0:T(8,128)}), f32[1024,512]{1,0:T(8,128)}) %all-gather.11.cloned.1.call-update) | async-done | bytes 2097168 | tf_op jit(solution)/shard_map/all_gather | solution.py:15
  115.8 42.0 %all-gather.9.cloned.1.call-done = f32[1024,512]{1,0:T(8,128)} async-done(((f32[64,512]{1,0:T(8,128)}), f32[1024,512]{1,0:T(8,128)}) %all-gather.9.cloned.1.call-update) | async-done | bytes 2097168 | tf_op jit(solution)/shard_map/all_gather | solution.py:15
  158.8 16.6 %while.35 = (s32[]{:T(128)}, f32[64,512]{1,0:T(8,128)S(1)}, f32[64,512]{1,0:T(8,128)S(1)}, f32[16,64,512]{2,1,0:T(8,128)}, f32[16,64,512]{2,1,0:T(8,128)}, /*index=5*/s32[]{:T(128)}, s32[]{:T(128)}, s32[]{:T(128)}) while((s32[]{:T(128)}, f32[64,512]{1,0:T(8,128)S(1)}, f32[64,512]{1,0:T(8,128)S(1)}, f32[16,64,512]{2,1,0:T(8,128)}, ...), condition=%wide.region_9.10_spmd, body=%wide.region_8.9_spmd.sunk | while | flops 196613 | bytes 786563 | solution.py:20
  158.8 1.1 fusion.28
  159.9 1.1 fusion.28
  161.0 1.1 fusion.28
  162.1 1.1 fusion.28
  168.8 1.1 fusion.28
  169.9 1.1 fusion.28
  171.0 1.1 fusion.28
  172.1 1.1 fusion.28
  173.2 1.1 fusion.28
  174.3 1.1 fusion.28
  175.4 15.3 %fusion.2 = f32[512,256]{0,1:T(8,128)S(1)} fusion(f32[64,512,256]{1,2,0:T(8,128)} %get-tuple-element.303, f32[64,512]{1,0:T(8,128)S(1)} %get-tuple-element.271, f32[64,512]{1,0:T(8,128)S(1)} %get-tuple-element.270, pred[512,256]{0,1:T(8,128)(4,1)S(1)} %copy.34), kind=kLoop, calls=%fused_computation.11 | loop fusion | flops 50200576 | bytes 34471936 | tf_op jit(solution)/shard_map/reduce_sum | solution.py:58
  191.8 38.9 %all-reduce.6.cloned.1.call-done = (f32[512,256]{1,0:T(8,128)}, f32[512,256]{1,0:T(8,128)}) async-done(((f32[512,256]{1,0:T(8,128)}, f32[512,256]{1,0:T(8,128)}), (f32[512,256]{1,0:T(8,128)}, f32[512,256]{1,0:T(8,128)})) %all-reduce.6.cloned.1.call-update) | async-done | bytes 1048592 | tf_op jit(solution)/shard_map/psum | solution.py:65
  230.7 1.3 fusion.14
  232.0 1.3 select_reduce_fusion.1
  233.4 21.4 %all-gather.5 = f32[16,1,512]{2,1,0:T(1,128)S(1)} all-gather(f32[1,1,512]{2,1,0:T(1,128)S(1)} %bitcast.75), channel_id=3, replica_groups=mesh['head'=2,'ctx'=16] {'ctx'}, dimensions={0}, use_global_device_ids=true | all-gather | bytes 34816 | tf_op jit(solution)/shard_map/all_gather | solution.py:15
  254.8 17.7 %all-gather.4 = f32[16,1,512]{2,1,0:T(1,128)S(1)} all-gather(f32[1,1,512]{2,1,0:T(1,128)S(1)} %bitcast.74), channel_id=2, replica_groups=mesh['head'=2,'ctx'=16] {'ctx'}, dimensions={0}, use_global_device_ids=true | all-gather | bytes 34816 | tf_op jit(solution)/shard_map/all_gather | solution.py:15
  273.3 1.5 multiply_subtract_fusion
  274.8 9.3 %fusion.11 = f32[256,128]{1,0:T(8,128)} fusion(u32[512,256]{1,0:T(8,128)S(1)} %get-tuple-element.300, f32[512,256]{1,0:T(8,128)S(1)} %multiply_subtract_fusion, f32[512,32]{0,1:T(8,128)S(1)} %copy-done.2, bf16[512,4096]{1,0:T(8,128)(2,1)} %param.13), kind=kOutput, calls=%fused_computation.24 | convolution fusion | flops 1103101952 | bytes 5439488 | tf_op jit(solution)/shard_map/tjs,tjd->sd/dot_general | solution.py:71
  284.2 7.5 %fusion.5 = f32[512,32,128]{0,2,1:T(8,128)} fusion(u32[512,256]{1,0:T(8,128)S(1)} %get-tuple-element.300, f32[512,256]{1,0:T(8,128)S(1)} %multiply_subtract_fusion, f32[512,32]{0,1:T(8,128)S(1)} %copy-done.2, bf16[256,128]{1,0:T(8,128)(2,1)S(1)} %copy-done), kind=kOutput, calls=%fused_computation.18 | convolution fusion | flops 1103101952 | bytes 9568256 | tf_op jit(solution)/shard_map/tjs,sd->tjd/dot_general | solution.py:75
  291.7 9.0 %copy.39 = f32[512,4096]{1,0:T(8,128)} copy(f32[512,4096]{0,1:T(8,128)} %bitcast.64) | data formatting | bytes 16777216 | tf_op jit(solution)/shard_map/reshape | solution.py:77
  300.7 2.6 all-reduce.4.cloned.1.call-done
  303.3 108.0 %reduce-scatter.2.cloned.1.call-done = f32[32,4096]{1,0:T(8,128)} async-done(((f32[512,4096]{1,0:T(8,128)}), f32[32,4096]{1,0:T(8,128)}) %reduce-scatter.2.cloned.1.call-update) | async-done | bytes 524304 | tf_op jit(solution)/shard_map/reduce_scatter | solution.py:76
  411.3 1.6 copy.85
  (64 shorter events, 12.3 us)
Async XLA Ops:
  7.2 64.2 %copy-start = (bf16[256,128]{1,0:T(8,128)(2,1)S(1)}, bf16[256,128]{1,0:T(8,128)(2,1)}, u32[]{:S(2)}) copy-start(bf16[256,128]{1,0:T(8,128)(2,1)} %param.14) | copy-start | bytes 196612
  7.2 107.7 %all-gather.11.cloned.1.call-start = ((), (), s32[]{:S(2)}) async-start(), calls=%async_computation.4 | async-start | bytes 2228224 | tf_op jit(solution)/shard_map/all_gather | solution.py:15
  55.0 15.6 %copy-start.1 = (f32[64,512]{1,0:T(8,128)}, f32[64,512]{1,0:T(8,128)S(1)}, u32[]{:S(2)}) copy-start(f32[64,512]{1,0:T(8,128)S(1)} %get-tuple-element.302) | copy-start | bytes 393220
  70.5 6.2 %copy-start.2 = (f32[512,32]{0,1:T(8,128)S(1)}, f32[512,32]{0,1:T(8,128)}, u32[]{:S(2)}) copy-start(f32[512,32]{0,1:T(8,128)} %param.15) | copy-start | bytes 196612
  70.6 87.3 %all-gather.9.cloned.1.call-start = ((), (), s32[]{:S(2)}) async-start(), calls=%async_computation.3 | async-start | bytes 2228224 | tf_op jit(solution)/shard_map/all_gather | solution.py:15
  71.3 159.4 %all-reduce.6.cloned.1.call-start = ((), (), s32[]{:S(2)}) async-start(), calls=%async_computation.5 | async-start | bytes 2097152 | tf_op jit(solution)/shard_map/psum | solution.py:65
  175.4 55.3 %copy-start.3 = (s32[512]{0:T(512)S(1)}, s32[512]{0:T(512)}, u32[]{:S(2)}) copy-start(s32[512]{0:T(512)} %param.16) | copy-start | bytes 6148
  191.8 111.6 %all-reduce.4.cloned.1.call-start = ((), (), s32[]{:S(2)}) async-start(), calls=%async_computation.2 | async-start | bytes 262144 | tf_op jit(solution)/shard_map/psum | solution.py:74
  284.2 127.1 %reduce-scatter.2.cloned.1.call-start = ((), (), s32[]{:S(2)}) async-start(), calls=%async_computation.1 | async-start | bytes 8912896 | tf_op jit(solution)/shard_map/reduce_scatter | solution.py:76
Sparse Core Ops, SparseCore 0:
  70.7 44.1 all-gather.10
  117.6 40.1 all-gather.8
  191.9 38.8 all-reduce.5
  284.3 18.9 all-reduce.3
  307.8 103.4 reduce-scatter.1
where the time goes:
time: 421 us; the launch traced here: 419 us
  waiting for transfers between devices  227 us (54%)
  other arithmetic  56.8 us (13%)
  matrix products  42.8 us (10%)
  local copies, waits for them, and re-layouts  39.1 us (9%)
  blocking collectives  39.1 us (9%)
  between operations  13.9 us (3%)
    reduce_scatter x1, waiting for transfers between devices, shards(): lax.psum_scatter(result.reshape(query_rows // lax.axis_size('ctx') * lax....  108 us
    all_gather x2, waiting for transfers between devices, combined_all(): gathered = jax.tree.map(lambda a: lax.all_gather(a, axis), part)  76.5 us
    all_gather x2, blocking collectives, combined_all(): gathered = jax.tree.map(lambda a: lax.all_gather(a, axis), part)  39.1 us
    psum x1, waiting for transfers between devices, shards(): target = lax.psum(target_part, 'head') / HEADS  38.9 us
    unnamed x13, local copies, waits for them, and re-layouts  27 us
    dot_general x1, matrix products, shards(): jnp.einsum('thd,shd->hts', query_heads, key_heads, preferred_element_type...  20.6 us
    reduce_sum x2, other arithmetic, row_stats(): jnp.sum(jnp.where(visible, jnp.exp(masked - local_top[..., None]), 0.0),...  16.9 us
    add x30, other arithmetic, combine_stats(): earlier[1] * jnp.exp(earlier[0] - top_value)  16.6 us
  transfers between devices with their start and end apart: 5, of which 5 were waited for; matrix products, arithmetic and copies ran while one was open for 6% of the time, Pallas kernels for 0%

commit v1 on v0

--- a/solution.py
+++ b/solution.py
@@ -62,7 +62,7 @@
         * inv_scale
     )
     logit_part = jnp.sum(head_weights[:, :, None] * jnp.maximum(activation, 0.0), axis=1)
-    target = lax.psum(target_part, "head") / HEADS
+    target = jnp.sum(lax.all_gather(target_part, "head"), axis=0) / HEADS
     logits = lax.psum(logit_part, "head")
     prob_step = row_stats(logits, visible) - target
     grad_terms = jnp.where(

time: 421 us -> 365 us (0.87)
  waiting for transfers between devices: 227 us -> 165 us
    psum x1, waiting for transfers between devices: 38.9 us -> 0.02 us  [shards(): logits = lax.psum(logit_part, 'head')]
    all_gather x2, waiting for transfers between devices: 76.5 us -> 42 us  [combined_all(): gathered = jax.tree.map(lambda a: lax.all_gather(a, axis), part)]
    all_gather x0 -> x1, waiting for transfers between devices: none -> 19.1 us  [shards(): target = jnp.sum(lax.all_gather(target_part, 'head'), axis=0) / HEADS]
    reduce_scatter x1, waiting for transfers between devices: 108 us -> 98.4 us  [shards(): lax.psum_scatter(result.reshape(query_rows // lax.axis_size('ctx') * lax....]
    unnamed x13 -> x17, local copies, waits for them, and re-layouts: 27 us -> 27.7 us
  transfers between devices with their start and end apart: 5 -> 6, of which waited for: 5 -> 5; matrix products, arithmetic and copies ran while one was open for 6% -> 23% of each run, Pallas kernels for 0% -> 0%
where the time goes in v1:
time: 365 us; the launch traced here: 363 us
  waiting for transfers between devices  165 us (45%)
  other arithmetic  56.3 us (15%)
  matrix products  42.9 us (12%)
  local copies, waits for them, and re-layouts  41.2 us (11%)
  blocking collectives  41 us (11%)
  between operations  15.6 us (4%)
    reduce_scatter x1, waiting for transfers between devices, shards(): lax.psum_scatter(result.reshape(query_rows // lax.axis_size('ctx') * lax....  98.4 us
    all_gather x2, waiting for transfers between devices, combined_all(): gathered = jax.tree.map(lambda a: lax.all_gather(a, axis), part)  42 us
    all_gather x2, blocking collectives, combined_all(): gathered = jax.tree.map(lambda a: lax.all_gather(a, axis), part)  41 us
    unnamed x17, local copies, waits for them, and re-layouts  27.7 us
    dot_general x1, matrix products, shards(): jnp.einsum('thd,shd->hts', query_heads, key_heads, preferred_element_type...  20.6 us
    all_gather x1, waiting for transfers between devices, shards(): target = jnp.sum(lax.all_gather(target_part, 'head'), axis=0) / HEADS  19.1 us
    reduce_sum x2, other arithmetic, row_stats(): jnp.sum(jnp.where(visible, jnp.exp(masked - local_top[..., None]), 0.0),...  16.9 us
    add x30, other arithmetic, combine_stats(): earlier[1] * jnp.exp(earlier[0] - top_value)  16.6 us
  transfers between devices with their start and end apart: 6, of which 5 were waited for; matrix products, arithmetic and copies ran while one was open for 23% of the time, Pallas kernels for 0%

profile of v1, /device:TPU:0, one launch (start us, length us, event | category | flops | bytes accessed | tf_op | source)
XLA Modules:
  0.0 363.3 jit_solution(15889245300614169870)
XLA Ops:
  8.8 5.3 %convert_reduce_fusion = (u32[512,256]{1,0:T(8,128)S(1)}, f32[512,32,256]{2,0,1:T(8,128)S(1)}) fusion(bf16[256,128]{1,0:T(8,128)(2,1)S(1)} %copy-done, bf16[512,4096]{1,0:T(8,128)(2,1)} %param.13), kind=kOutput, calls=%fused_computation.14 | convolution fusion | flops 1094582272 | bytes 21561344 | tf_op jit(solution)/shard_map/tjd,sd->tjs/dot_general | solution.py:61
  14.2 3.7 %multiply_reduce_fusion = f32[512,256]{1,0:T(8,128)} fusion(f32[512,32,256]{2,0,1:T(8,128)S(1)} %get-tuple-element.299, f32[512,32]{0,1:T(8,128)S(1)} %copy-done.3), kind=kLoop, calls=%fused_computation.16 | loop fusion | flops 16646144 | bytes 17367040 | tf_op jit(solution)/shard_map/reduce_sum | solution.py:64
  18.4 16.7 %copy.43 = bf16[512,12288]{0,1:T(8,128)(2,1)} copy(bf16[512,12288]{1,0:T(8,128)(2,1)} %param.11) | data formatting | bytes 25165824 | tf_op args[0]
  35.0 8.7 %copy.44 = bf16[256,12288]{0,1:T(8,128)(2,1)} copy(bf16[256,12288]{1,0:T(8,128)(2,1)} %param.12) | data formatting | bytes 12582912 | tf_op args[1]
  43.7 20.6 %fusion.3 = (f32[64,512]{1,0:T(8,128)S(1)}, f32[64,512,256]{1,2,0:T(8,128)}) fusion(pred[512,256]{0,1:T(8,128)(4,1)S(1)} %copy.42, bf16[512,64,192]{0,2,1:T(8,128)(2,1)} %bitcast.65, bf16[256,64,192]{0,2,1:T(8,128)(2,1)} %bitcast.67), kind=kOutput, calls=%fused_computation.12 | convolution fusion | flops 3246358528 | bytes 52690944 | tf_op jit(solution)/shard_map/thd,shd->hts/dot_general | solution.py:54
  64.4 15.6 %select_reduce_fusion = f32[64,512]{1,0:T(8,128)} fusion(f32[64,512,256]{1,2,0:T(8,128)} %get-tuple-element.301, f32[64,512]{1,0:T(8,128)S(1)} %get-tuple-element.300, pred[512,256]{0,1:T(8,128)(4,1)S(1)} %copy.42), kind=kLoop, calls=%fused_computation.9 | loop fusion | flops 41910272 | bytes 33947648 | tf_op jit(solution)/shard_map/reduce_sum | solution.py:36
  80.6 1.3 fusion.14
  81.9 1.3 select_reduce_fusion.1
  83.3 23.3 %all-gather.6 = f32[16,1,512]{2,1,0:T(1,128)S(1)} all-gather(f32[1,1,512]{2,1,0:T(1,128)S(1)} %bitcast.77), channel_id=3, replica_groups=mesh['head'=2,'ctx'=16] {'ctx'}, dimensions={0}, use_global_device_ids=true | all-gather | bytes 34816 | tf_op jit(solution)/shard_map/all_gather | solution.py:15
  106.6 17.7 %all-gather.5 = f32[16,1,512]{2,1,0:T(1,128)S(1)} all-gather(f32[1,1,512]{2,1,0:T(1,128)S(1)} %bitcast.76), channel_id=2, replica_groups=mesh['head'=2,'ctx'=16] {'ctx'}, dimensions={0}, use_global_device_ids=true | all-gather | bytes 34816 | tf_op jit(solution)/shard_map/all_gather | solution.py:15
  125.3 41.9 %all-gather.11.cloned.1.call-done = f32[1024,512]{1,0:T(8,128)} async-done(((f32[64,512]{1,0:T(8,128)}), f32[1024,512]{1,0:T(8,128)}) %all-gather.11.cloned.1.call-update) | async-done | bytes 2097168 | tf_op jit(solution)/shard_map/all_gather | solution.py:15
  168.1 16.6 %while.35 = (s32[]{:T(128)}, f32[64,512]{1,0:T(8,128)S(1)}, f32[64,512]{1,0:T(8,128)S(1)}, f32[16,64,512]{2,1,0:T(8,128)}, f32[16,64,512]{2,1,0:T(8,128)}, /*index=5*/s32[]{:T(128)}, s32[]{:T(128)}, s32[]{:T(128)}) while((s32[]{:T(128)}, f32[64,512]{1,0:T(8,128)S(1)}, f32[64,512]{1,0:T(8,128)S(1)}, f32[16,64,512]{2,1,0:T(8,128)}, ...), condition=%wide.region_9.10_spmd, body=%wide.region_8.9_spmd.sunk | while | flops 196613 | bytes 786563 | solution.py:20
  168.1 1.1 fusion.28
  169.2 1.1 fusion.28
  171.4 1.1 fusion.28
  172.5 1.1 fusion.28
  173.6 1.1 fusion.28
  175.9 1.1 fusion.28
  177.0 1.1 fusion.28
  178.1 1.1 fusion.28
  180.3 1.1 fusion.28
  181.4 1.1 fusion.28
  184.7 16.2 %fusion.2 = f32[512,256]{0,1:T(8,128)} fusion(f32[64,512,256]{1,2,0:T(8,128)} %get-tuple-element.301, f32[64,512]{1,0:T(8,128)S(1)} %get-tuple-element.271, f32[64,512]{1,0:T(8,128)S(1)} %get-tuple-element.270, pred[512,256]{0,1:T(8,128)(4,1)S(1)} %copy.42), kind=kLoop, calls=%fused_computation.11 | loop fusion | flops 50200576 | bytes 34471936 | tf_op jit(solution)/shard_map/reduce_sum | solution.py:58
  202.0 19.1 %all-gather.15.cloned.1.call-done = f32[1024,256]{0,1:T(8,128)} async-done(((f32[512,256]{0,1:T(8,128)}), f32[1024,256]{0,1:T(8,128)}) %all-gather.15.cloned.1.call-update) | async-done | bytes 1048592 | tf_op jit(solution)/shard_map/all_gather | solution.py:65
  221.1 2.1 reshape.57
  223.2 1.2 reduce_sum.49
  224.9 9.4 %fusion.11 = f32[256,128]{1,0:T(8,128)} fusion(u32[512,256]{1,0:T(8,128)S(1)} %get-tuple-element.298, f32[512,256]{1,0:T(8,128)S(1)} %multiply_subtract_fusion, f32[512,32]{0,1:T(8,128)S(1)} %copy-done.3, bf16[512,4096]{1,0:T(8,128)(2,1)} %param.13), kind=kOutput, calls=%fused_computation.24 | convolution fusion | flops 1103101952 | bytes 5439488 | tf_op jit(solution)/shard_map/tjs,tjd->sd/dot_general | solution.py:71
  234.4 7.5 %fusion.5 = f32[512,32,128]{0,2,1:T(8,128)} fusion(u32[512,256]{1,0:T(8,128)S(1)} %get-tuple-element.298, f32[512,256]{1,0:T(8,128)S(1)} %multiply_subtract_fusion, f32[512,32]{0,1:T(8,128)S(1)} %copy-done.3, bf16[256,128]{1,0:T(8,128)(2,1)S(1)} %copy-done), kind=kOutput, calls=%fused_computation.18 | convolution fusion | flops 1103101952 | bytes 9568256 | tf_op jit(solution)/shard_map/tjs,sd->tjd/dot_general | solution.py:75
  241.9 9.0 %copy.47 = f32[512,4096]{1,0:T(8,128)} copy(f32[512,4096]{0,1:T(8,128)} %bitcast.66) | data formatting | bytes 16777216 | tf_op jit(solution)/shard_map/reshape | solution.py:77
  250.9 5.2 %all-reduce.5.cloned.1.call-done = f32[256,128]{1,0:T(8,128)} async-done(((f32[256,128]{1,0:T(8,128)}), f32[256,128]{1,0:T(8,128)}) %all-reduce.5.cloned.1.call-update) | async-done | bytes 131088 | tf_op jit(solution)/shard_map/psum | solution.py:74
  256.0 98.4 %reduce-scatter.2.cloned.1.call-done = f32[32,4096]{1,0:T(8,128)} async-done(((f32[512,4096]{1,0:T(8,128)}), f32[32,4096]{1,0:T(8,128)}) %reduce-scatter.2.cloned.1.call-update) | async-done | bytes 524304 | tf_op jit(solution)/shard_map/reduce_scatter | solution.py:76
  354.4 1.6 copy.92
  (73 shorter events, 11.5 us)
Async XLA Ops:
  8.0 0.8 copy-start
  8.0 6.2 %copy-start.3 = (f32[512,32]{0,1:T(8,128)S(1)}, f32[512,32]{0,1:T(8,128)}, u32[]{:S(2)}) copy-start(f32[512,32]{0,1:T(8,128)} %param.15) | copy-start | bytes 196612
  8.0 9.9 %copy-start.5 = (s32[256]{0:T(256)S(1)}, s32[256]{0:T(256)}, u32[]{:S(2)}) copy-start(s32[256]{0:T(256)} %param.17) | copy-start | bytes 3076
  8.0 9.9 %copy-start.4 = (s32[512]{0:T(512)S(1)}, s32[512]{0:T(512)}, u32[]{:S(2)}) copy-start(s32[512]{0:T(512)} %param.16) | copy-start | bytes 6148
  8.0 72.6 %all-reduce.3.cloned.1.call-start = ((), (), s32[]{:S(2)}) async-start(), calls=%async_computation.1 | async-start | bytes 1048576 | tf_op jit(solution)/shard_map/psum | solution.py:66
  17.9 106.5 %all-gather.13.cloned.1.call-start = ((), (), s32[]{:S(2)}) async-start(), calls=%async_computation.5 | async-start | bytes 2228224 | tf_op jit(solution)/shard_map/all_gather | solution.py:15
  64.4 15.6 %copy-start.2 = (f32[64,512]{1,0:T(8,128)}, f32[64,512]{1,0:T(8,128)S(1)}, u32[]{:S(2)}) copy-start(f32[64,512]{1,0:T(8,128)S(1)} %get-tuple-element.300) | copy-start | bytes 393220
  80.0 87.2 %all-gather.11.cloned.1.call-start = ((), (), s32[]{:S(2)}) async-start(), calls=%async_computation.4 | async-start | bytes 2228224 | tf_op jit(solution)/shard_map/all_gather | solution.py:15
  80.6 140.5 %all-gather.15.cloned.1.call-start = ((), (), s32[]{:S(2)}) async-start(), calls=%async_computation.6 | async-start | bytes 1572864 | tf_op jit(solution)/shard_map/all_gather | solution.py:65
  184.7 39.9 %copy-start.1 = (f32[512,256]{1,0:T(8,128)S(1)}, f32[512,256]{1,0:T(8,128)}, u32[]{:S(2)}) copy-start(f32[512,256]{1,0:T(8,128)} %all-reduce.3.cloned.1.call-done) | copy-start | bytes 1572868
  200.9 55.1 %all-reduce.5.cloned.1.call-start = ((), (), s32[]{:S(2)}) async-start(), calls=%async_computation.3 | async-start | bytes 262144 | tf_op jit(solution)/shard_map/psum | solution.py:74
  234.3 120.1 %reduce-scatter.2.cloned.1.call-start = ((), (), s32[]{:S(2)}) async-start(), calls=%async_computation.2 | async-start | bytes 8912896 | tf_op jit(solution)/shard_map/reduce_scatter | solution.py:76
Sparse Core Ops, SparseCore 0:
  18.0 31.3 all-reduce.2
  201.0 20.0 all-gather.14
  234.4 21.5 all-reduce.4
Sparse Core Ops, SparseCore 1:
  80.1 44.3 all-gather.12
  127.0 40.1 all-gather.10
  250.9 103.4 reduce-scatter.1
